TPU v7x, 128 devices: a whole 4x4x4 slice. The times are simulated.
128 devices in a mesh: lat: 8 (over z, core), lon: 16 (over x, y).
Axes of the slice: x: 4, y: 4, z: 4, core: 2. Of those that a mesh axis runs over, the one named last changes fastest.
Arguments:
- patches: bfloat16 [24576, 1536], P(('lat', 'lon')), may hold values from -6 to 6
- requests: int32 [8, 8192], P('lat', 'lon'), may hold values from 0 to 191, as said below
- footprint: int32 [512, 128], P('lat', 'lon'), may hold values from -1 to 511, as said below
- weight_index: int32 [512, 128], P('lat', 'lon'), may hold values from 0 to 15
- composite_weights: float32 [16], replicated, may hold values from 0.1 to 1
- labels: int32 [512, 2048], P('lat', 'lon'), may hold values from 0 to 10
- conv1_weight: bfloat16 [9, 64, 12], replicated, may hold values from -0.625 to 0.625
- conv2_weight: bfloat16 [9, 64, 64], replicated, may hold values from -0.25 to 0.25
- head_weight: bfloat16 [11, 64], replicated, may hold values from -0.75 to 0.75
Outputs:
- skip_features: bfloat16 [64, 512, 2048], P(None, 'lat', 'lon')
- grad_conv1: float32 [9, 64, 12], replicated
- grad_conv2: float32 [9, 64, 64], replicated
- grad_head: float32 [11, 64], replicated
- loss: float32 [], replicated
Inputs may be any that keep to these rules, and one draw needn't show every extreme that they name: `requests`: every entry is a row offset into the store of the device at the same lat index and lon index b. `footprint`: an entry that is not -1 is b*32 + p, position p of the bucket that the tile takes from lon index b. Slot 0 is never -1. In one tile no two entries are equal, and in some tiles every position of every bucket is named.
All inputs are finite; a program needn't handle non-finite values.
Results may differ from a plain program's by a relative error of at most 0.0055.
Values may be sent and summed in bfloat16 or wider, within the bound.
A program may use at most 64 MiB of HBM per device.

v0:
```python
import functools

import jax
import jax.numpy as jnp
from jax import lax
from jax.experimental import pallas as pl
from jax.experimental.pallas import tpu as pltpu
from jax.sharding import PartitionSpec as P

F32 = jnp.float32
BF16 = jnp.bfloat16
NLAT, NLON = 8, 16
ROWS, COLS, BANDS, FEAT, NCLASS, SLOTS, BUCKET, STORE = 64, 128, 12, 64, 11, 8, 32, 192
WIDTH = BANDS * COLS
CHUNKS = 3
CW = WIDTH // CHUNKS
MESH = pl.DeviceIdType.MESH
VM = pl.BlockSpec(memory_space=pltpu.VMEM)


def lane_iota(shape):
    return lax.broadcasted_iota(jnp.int32, shape, len(shape) - 1)


def dot_nt(a, b):
    return lax.dot_general(a, b, (((1,), (1,)), ((), ())), preferred_element_type=F32)


def dot_tn(a, b):
    return lax.dot_general(a, b, (((0,), (0,)), ((), ())), preferred_element_type=F32)


def dot(a, b):
    return jnp.dot(a, b, preferred_element_type=F32)


def gather_kernel(
    patches, requests, foot, widx, cw, labels, comp, strip,
    reqs, hot, sendbuf, recv, bands, picked, hsend, from_up, from_down, side,
    req_send, req_recv, row_send, row_recv, halo_send, halo_recv,
):
    lat, lon = lax.axis_index("lat"), lax.axis_index("lon")
    up, down = lax.rem(lat + NLAT - 1, NLAT), lax.rem(lat + 1, NLAT)
    left, right = lax.rem(lon + NLON - 1, NLON), lax.rem(lon + 1, NLON)

    barrier = pltpu.get_barrier_semaphore()

    def greet(k, _):
        peer = lax.rem(lon + k, NLON)
        pl.semaphore_signal(barrier, inc=1, device_id=(lat, peer), device_id_type=MESH)
        return 0

    lax.fori_loop(1, NLON, greet, 0)
    for i in (up, down):
        for d in (left, lon, right):
            pl.semaphore_signal(barrier, inc=1, device_id=(i, d), device_id_type=MESH)
    pl.semaphore_wait(barrier, NLON - 1 + 6)

    def req_copy(k, peer):
        start = pl.multiple_of((peer // 4) * 128, 128)
        return pltpu.make_async_remote_copy(
            src_ref=requests.at[:, pl.ds(start, 128)], dst_ref=reqs.at[lon],
            send_sem=req_send.at[k], recv_sem=req_recv.at[lon],
            device_id=(lat, peer), device_id_type=MESH)

    def req_arrival(source):
        return pltpu.make_async_remote_copy(
            src_ref=requests.at[:, pl.ds(0, 128)], dst_ref=reqs.at[source],
            send_sem=req_send.at[0], recv_sem=req_recv.at[source],
            device_id=(lat, lon), device_id_type=MESH)

    def send_req(k, _):
        req_copy(k, lax.rem(lon + k, NLON)).start()
        return 0

    lax.fori_loop(1, NLON, send_req, 0)
    own = pl.multiple_of((lon // 4) * 128, 128)
    reqs[lon] = requests[:, pl.ds(own, 128)]

    level = widx[...]
    weight = jnp.zeros((ROWS, SLOTS), F32)
    for q in range(16):
        weight = jnp.where(level == q, cw[q], weight)
    entry = foot[...]
    weight = jnp.where(entry >= 0, weight, 0.0)
    total = jnp.sum(weight, axis=1, keepdims=True)
    position = lane_iota((ROWS, NLON * BUCKET))
    blend = jnp.zeros((ROWS, NLON * BUCKET), F32)
    for k in range(SLOTS):
        blend = blend + jnp.where(entry[:, k : k + 1] == position, weight[:, k : k + 1], 0.0)
    blend_hi = blend.astype(BF16)
    blend_lo = (blend - blend_hi.astype(F32)).astype(BF16)

    def wait_req(k, _):
        req_arrival(lax.rem(lon + k, NLON)).wait_recv()
        return 0

    lax.fori_loop(1, NLON, wait_req, 0)

    lanes = lane_iota((1, 128))
    base = 32 * lax.rem(lon, 4)
    store_row = lax.broadcasted_iota(jnp.int32, (STORE, 128), 0)
    for t in range(4):
        asked = jnp.zeros((1, 128), jnp.int32)
        for j in range(4):
            turned = pltpu.roll(reqs[4 * t + j], lax.rem(32 * j - base + 128, 128), 1)
            asked = jnp.where((lanes >= 32 * j) & (lanes < 32 * j + 32), turned, asked)
        hot[:, 128 * t : 128 * (t + 1)] = jnp.where(store_row == asked, 1.0, 0.0).astype(BF16)

    def row_copy(c, k, peer):
        return pltpu.make_async_remote_copy(
            src_ref=sendbuf.at[c, peer], dst_ref=recv.at[c, lon],
            send_sem=row_send.at[c, k], recv_sem=row_recv.at[c, lon],
            device_id=(lat, peer), device_id_type=MESH)

    def row_arrival(c, source):
        return pltpu.make_async_remote_copy(
            src_ref=sendbuf.at[c, source], dst_ref=recv.at[c, source],
            send_sem=row_send.at[c, 0], recv_sem=row_recv.at[c, source],
            device_id=(lat, lon), device_id_type=MESH)

    for c in range(CHUNKS):
        rows = dot_tn(hot[...], patches[:, c * CW : (c + 1) * CW]).astype(BF16)
        sendbuf[c] = rows.reshape(NLON, BUCKET, CW)

        def send_rows(k, _):
            row_copy(c, k, lax.rem(lon + k, NLON)).start()
            return 0

        lax.fori_loop(1, NLON, send_rows, 0)
        recv[c, lon] = sendbuf[c, lon]

    for k in range(BANDS + 1, 16):
        bands[k] = jnp.zeros((ROWS, COLS), F32)
    bands[BANDS] = labels[...].astype(F32)
    for c in range(CHUNKS):

        def wait_rows(k, _):
            row_arrival(c, lax.rem(lon + k, NLON)).wait_recv()
            return 0

        lax.fori_loop(1, NLON, wait_rows, 0)
        rows = recv[c].reshape(NLON * BUCKET, CW)
        blended = (dot(blend_hi, rows) + dot(blend_lo, rows)) / total
        blended = blended.astype(BF16).astype(F32)
        for b in range(CW // COLS):
            bands[c * (CW // COLS) + b] = blended[:, b * COLS : (b + 1) * COLS]

    pick_row = lax.broadcasted_iota(jnp.int32, (8, COLS), 0)
    pick_lane = lane_iota((8, COLS))
    pick = jnp.where(pick_lane == jnp.where(pick_row < 3, pick_row, pick_row + 122), 1.0, 0.0)
    columns = dot_nt(pick.astype(BF16), bands[...].reshape(16 * ROWS, COLS).astype(BF16))
    for k in range(16):
        picked[k] = jnp.concatenate(
            [columns[:, k * ROWS : (k + 1) * ROWS], jnp.zeros((8, 64), F32)], axis=1)
    for x in range(3):
        hsend[3 + x] = picked[:, x, :].astype(BF16)
        hsend[6 + x] = picked[:, 3 + x, :].astype(BF16)
    for r in range(3):
        hsend[r] = bands[:, r, :].astype(BF16)
        hsend[9 + r] = bands[:, ROWS - 3 + r, :].astype(BF16)

    def halo_copies():
        made = [
            (hsend.at[0:9], from_down, (up, lon)),
            (hsend.at[3:12], from_up, (down, lon)),
            (hsend.at[3:6], side.at[3], (lat, left)),
            (hsend.at[6:9], side.at[0], (lat, right)),
            (hsend.at[3:6], side.at[5], (up, left)),
            (hsend.at[6:9], side.at[2], (up, right)),
            (hsend.at[3:6], side.at[4], (down, left)),
            (hsend.at[6:9], side.at[1], (down, right)),
        ]
        return [
            pltpu.make_async_remote_copy(
                src_ref=s, dst_ref=d, send_sem=halo_send.at[n], recv_sem=halo_recv.at[n],
                device_id=who, device_id_type=MESH)
            for n, (s, d, who) in enumerate(made)
        ]

    copies = halo_copies()
    for copy in copies:
        copy.start()

    for r in range(ROWS):
        comp[3 + r] = bands[:, r, :].astype(BF16)

    for copy in copies:
        copy.wait_recv()

    has_up, has_down = lat > 0, lat < NLAT - 1
    has_left, has_right = lon > 0, lon < NLON - 1
    for r in range(3):
        comp[r] = jnp.where(has_up, from_up[6 + r].astype(F32), 0.0).astype(BF16)
        comp[67 + r] = jnp.where(has_down, from_down[r].astype(F32), 0.0).astype(BF16)
    tile_lane = lane_iota((16, 128))

    def joined(middle, above, below, inside):
        turned = pltpu.roll(middle.astype(F32), 3, 1)
        result = jnp.where((tile_lane >= 3) & (tile_lane < 67), turned, 0.0)
        top = pltpu.roll(above.astype(F32), 67, 1)
        result = jnp.where((tile_lane < 3) & has_up, top, result)
        bottom = pltpu.roll(below.astype(F32), 67, 1)
        result = jnp.where((tile_lane >= 67) & (tile_lane < 70) & has_down, bottom, result)
        if inside is not None:
            result = jnp.where(inside, result, 0.0)
        return result.astype(BF16)

    for x in range(3):
        strip[x] = joined(side[0, x], side[1, x], side[2, x], has_left)
        strip[7 + x] = joined(side[3, x], side[4, x], side[5, x], has_right)
    for x in range(2):
        strip[3 + x] = joined(hsend[3 + x], from_up[x], from_down[3 + x], None)
        strip[5 + x] = joined(hsend[7 + x], from_up[4 + x], from_down[7 + x], None)

    for copy in copies:
        copy.wait_send()

    def drain(k, _):
        peer = lax.rem(lon + k, NLON)
        req_copy(k, peer).wait_send()
        for c in range(CHUNKS):
            row_copy(c, k, peer).wait_send()
        return 0

    lax.fori_loop(1, NLON, drain, 0)


def gather(patches, requests, foot, widx, cw, labels):
    return pl.pallas_call(
        gather_kernel,
        out_shape=(
            jax.ShapeDtypeStruct((70, 16, 128), BF16),
            jax.ShapeDtypeStruct((10, 16, 128), BF16),
        ),
        in_specs=[VM, VM, VM, VM, pl.BlockSpec(memory_space=pltpu.SMEM), VM],
        out_specs=(VM, VM),
        scratch_shapes=[
            pltpu.VMEM((NLON, 1, 128), jnp.int32),
            pltpu.VMEM((STORE, NLON * BUCKET), BF16),
            pltpu.VMEM((CHUNKS, NLON, BUCKET, CW), BF16),
            pltpu.VMEM((CHUNKS, NLON, BUCKET, CW), BF16),
            pltpu.VMEM((16, ROWS, COLS), F32),
            pltpu.VMEM((16, 8, 128), F32),
            pltpu.VMEM((12, 16, 128), BF16),
            pltpu.VMEM((9, 16, 128), BF16),
            pltpu.VMEM((9, 16, 128), BF16),
            pltpu.VMEM((6, 3, 16, 128), BF16),
            pltpu.SemaphoreType.DMA((NLON,)),
            pltpu.SemaphoreType.DMA((NLON,)),
            pltpu.SemaphoreType.DMA((CHUNKS, NLON)),
            pltpu.SemaphoreType.DMA((CHUNKS, NLON)),
            pltpu.SemaphoreType.DMA((8,)),
            pltpu.SemaphoreType.DMA((8,)),
        ],
        compiler_params=pltpu.CompilerParams(collective_id=0, has_side_effects=True),
        name="gather_blend_halo",
    )(patches, requests, foot, widx, cw, labels)


def sigmoid(v):
    return 0.5 * jnp.tanh(0.5 * v) + 0.5


def slope_of(v, s):
    return s * (1.0 + v * (1.0 - s))


def tile_kernel(
    comp, strip, w1, w2, head, skip_out, grads,
    w1k, w2k, w2a, x1, x2, x3, pre1, sk, edge, hid, skip3, acc2, acc1, acch, accl,
):
    lat, lon = lax.axis_index("lat"), lax.axis_index("lon")
    has_up, has_down = lat > 0, lat < NLAT - 1
    has_left, has_right = lon > 0, lon < NLON - 1

    w1k[...] = jnp.zeros_like(w1k)
    for t in range(9):
        w1k[:, 16 * t : 16 * t + BANDS] = w1[t]
        w2k[:, 64 * t : 64 * (t + 1)] = w2[t]
        w2a[:, 64 * t : 64 * (t + 1)] = w2[8 - t].astype(F32).T.astype(BF16)
    headp = jnp.concatenate(
        [head[...].astype(F32), jnp.zeros((16 - NCLASS, FEAT), F32)], axis=0).astype(BF16)

    def spread(dst, tile, index, tile_f32, left_col, right_col, lane_row, height):
        lanes = lane_iota((height, 128))
        put_left = pltpu.roll(left_col, lax.rem(128 - lane_row, 128), 1)
        put_right = pltpu.roll(right_col, lax.rem(255 - lane_row, 128), 1)
        at = pl.ds(pl.multiple_of(index * 128, 128), 128)
        dst[0:height, at] = jnp.where(lanes == 0, put_left, pltpu.roll(tile_f32, 1, 1)).astype(BF16)
        dst[height : 2 * height, at] = tile
        dst[2 * height : 3 * height, at] = jnp.where(
            lanes == 127, put_right, pltpu.roll(tile_f32, 127, 1)).astype(BF16)

    comp_left = strip[2].astype(F32)
    comp_right = strip[7].astype(F32)

    def spread_comp(i, _):
        for j in range(7):
            t = i * 7 + j
            tile = comp[t]
            spread(x1, tile, t, tile.astype(F32), comp_left, comp_right, t, 16)
        return 0

    lax.fori_loop(0, 10, spread_comp, 0)

    lanes16 = lane_iota((16, 128))
    del lanes16
    turned = [[pltpu.roll(strip[s].astype(F32), (128 - u) % 128, 1).astype(BF16) for u in (-1, 0, 1)]
              for s in range(10)]
    lanes64 = lane_iota((FEAT, 128))
    row_ok = ((lanes64 >= 3) | has_up) & ((lanes64 < 67) | has_down) & (lanes64 >= 1) & (lanes64 < 69)
    for n, s in enumerate((1, 2, 3, 6, 7, 8)):
        stack = jnp.concatenate([turned[s + v][u] for u in range(3) for v in (-1, 0, 1)], axis=0)
        pre = dot(w1k[...], stack)
        keep = row_ok
        if s in (1, 2):
            keep = keep & has_left
        if s in (7, 8):
            keep = keep & has_right
        hid[n] = jnp.where(keep, pre * sigmoid(pre), 0.0)
    hid_left = hid[1]
    hid_right = hid[4]

    def stack_of(ref, first, count):
        return jnp.concatenate(
            [ref[:, pl.ds(pl.multiple_of((first + u) * 128, 128), count * 128)] for u in (-1, 0, 1)],
            axis=0)

    for first, inside in ((1, has_up), (67, has_down)):
        pre = dot(w1k[...], stack_of(x1, first, 2))
        value = jnp.where(inside, pre * sigmoid(pre), 0.0)
        for j in range(2):
            tile = value[:, 128 * j : 128 * (j + 1)]
            spread(x2, tile.astype(BF16), first - 1 + j, tile, hid_left, hid_right, first + j, FEAT)

    def conv_one(i, _):
        first = i * 8
        pre = dot(w1k[...], stack_of(x1, first + 3, 8))
        pre1[:, pl.ds(pl.multiple_of(first * 128, 128), 1024)] = pre
        value = pre * sigmoid(pre)
        for j in range(8):
            tile = value[:, 128 * j : 128 * (j + 1)]
            spread(x2, tile.astype(BF16), first + 2 + j, tile, hid_left, hid_right, first + 3 + j, FEAT)
        return 0

    lax.fori_loop(0, 8, conv_one, 0)

    def head_of(pre, label):
        width = pre.shape[1]
        s = sigmoid(pre)
        skip = (pre * s).astype(BF16)
        logits = dot(headp, skip)
        classes = lax.broadcasted_iota(jnp.int32, (16, width), 0)
        power = jnp.where(classes < NCLASS, jnp.exp(logits), 0.0)
        total = jnp.sum(power, axis=0, keepdims=True)
        onehot = classes == label.astype(jnp.int32)
        error = (power / total - jnp.where(onehot, 1.0, 0.0)).astype(BF16)
        slope = dot_tn(headp, error) * slope_of(pre, s)
        loss = jnp.log(total) - jnp.sum(jnp.where(onehot, logits, 0.0), axis=0, keepdims=True)
        return skip, error, slope, loss

    edge[:, 0:128] = dot(w2k[...], stack_of(x2, 1, 1))
    edge[:, 128:256] = dot(w2k[...], stack_of(x2, 66, 1))
    for n, middle in enumerate((1, 4)):
        stack = jnp.concatenate(
            [pltpu.roll(hid[middle + v], (128 - u) % 128, 1).astype(BF16)
             for u in (-1, 0, 1) for v in (-1, 0, 1)], axis=0)
        edge[:, 256 + 128 * n : 384 + 128 * n] = dot(w2k[...], stack)

    def label_row(tile):
        return tile.astype(F32)[BANDS : BANDS + 1, :]

    edge_label = jnp.concatenate(
        [label_row(comp[2]), label_row(comp[67]), label_row(strip[2]), label_row(strip[7])], axis=1)
    _, _, edge_slope, _ = head_of(edge[...], edge_label)
    slope_left = jnp.where(row_ok & has_left, edge_slope[:, 256:384], 0.0)
    slope_right = jnp.where(row_ok & has_right, edge_slope[:, 384:512], 0.0)
    slope_top = jnp.where(has_up, edge_slope[:, 0:128], 0.0)
    slope_bottom = jnp.where(has_down, edge_slope[:, 128:256], 0.0)
    hid[0] = slope_left
    hid[2] = slope_right
    spread(x3, slope_top.astype(BF16), 0, slope_top, slope_left, slope_right, 2, FEAT)
    spread(x3, slope_bottom.astype(BF16), 65, slope_bottom, slope_left, slope_right, 67, FEAT)

    acc2[...] = jnp.zeros_like(acc2)
    acc1[...] = jnp.zeros_like(acc1)
    acch[...] = jnp.zeros_like(acch)
    accl[...] = jnp.zeros_like(accl)

    def conv_two(i, _):
        first = i * 8
        stack = stack_of(x2, first + 2, 8)
        pre = dot(w2k[...], stack)
        label = jnp.concatenate([label_row(comp[first + 3 + j]) for j in range(8)], axis=1)
        skip, error, slope, loss = head_of(pre, label)
        acch[...] += dot_nt(skip, error)
        accl[...] += loss
        skip_f32 = skip.astype(F32)
        left_col, right_col = hid[0], hid[2]
        for j in range(8):
            tile = slope[:, 128 * j : 128 * (j + 1)]
            spread(x3, tile.astype(BF16), first + 1 + j, tile, left_col, right_col, first + 3 + j, FEAT)
            skip3[:, j, :] = skip_f32[:, 128 * j : 128 * (j + 1)]
        skip_out[:, pl.ds(pl.multiple_of(first, 8), 8), :] = skip3[...].astype(BF16)
        acc2[...] += dot_nt(slope.astype(BF16), stack)
        return 0

    lax.fori_loop(0, 8, conv_two, 0)

    def back_one(i, _):
        first = i * 8
        back = dot(w2a[...], stack_of(x3, first + 1, 8))
        pre = pre1[:, pl.ds(pl.multiple_of(first * 128, 128), 1024)]
        slope = (back * slope_of(pre, sigmoid(pre))).astype(BF16)
        acc1[...] += dot_nt(slope, stack_of(x1, first + 3, 8))
        return 0

    lax.fori_loop(0, 8, back_one, 0)

    loss_total = jnp.sum(jnp.sum(accl[...], axis=1, keepdims=True), axis=0, keepdims=True)
    packed = jnp.concatenate(
        [acc2[...], acc1[...], acch[...], jnp.broadcast_to(loss_total, (FEAT, 32))], axis=1)
    for g in range(8):
        for h in range(6):
            grads[6 * g + h] = packed[8 * g : 8 * (g + 1), 128 * h : 128 * (h + 1)]


def tile_pass(comp, strip, w1, w2, head):
    return pl.pallas_call(
        tile_kernel,
        out_shape=(
            jax.ShapeDtypeStruct((FEAT, ROWS, COLS), BF16),
            jax.ShapeDtypeStruct((48, 8, 128), F32),
        ),
        in_specs=[VM] * 5,
        out_specs=(VM, VM),
        scratch_shapes=[
            pltpu.VMEM((64, 144), BF16),
            pltpu.VMEM((64, 576), BF16),
            pltpu.VMEM((64, 576), BF16),
            pltpu.VMEM((48, 70 * 128), BF16),
            pltpu.VMEM((192, 68 * 128), BF16),
            pltpu.VMEM((192, 66 * 128), BF16),
            pltpu.VMEM((64, 64 * 128), F32),
            pltpu.VMEM((8, 128), F32),
            pltpu.VMEM((64, 512), F32),
            pltpu.VMEM((6, 64, 128), F32),
            pltpu.VMEM((64, 8, 128), F32),
            pltpu.VMEM((64, 576), F32),
            pltpu.VMEM((64, 144), F32),
            pltpu.VMEM((64, 16), F32),
            pltpu.VMEM((1, 1024), F32),
        ],
        name="tile_forward_backward",
    )(comp, strip, w1, w2, head)


def sum_kernel(part, out, first, second, whole, s1, r1, s2, r2, s3, r3):
    lat, lon = lax.axis_index("lat"), lax.axis_index("lon")
    barrier = pltpu.get_barrier_semaphore()

    def greet_lon(k, _):
        pl.semaphore_signal(
            barrier, inc=1, device_id=(lat, lax.rem(lon + k, NLON)), device_id_type=MESH)
        return 0

    def greet_lat(k, _):
        pl.semaphore_signal(
            barrier, inc=1, device_id=(lax.rem(lat + k, NLAT), lon), device_id_type=MESH)
        return 0

    lax.fori_loop(1, NLON, greet_lon, 0)
    lax.fori_loop(1, NLAT, greet_lat, 0)
    pl.semaphore_wait(barrier, NLON - 1 + NLAT - 1)

    def scatter(k, peer, source):
        return pltpu.make_async_remote_copy(
            src_ref=part.at[pl.ds(3 * peer, 3)], dst_ref=first.at[source],
            send_sem=s1.at[k], recv_sem=r1.at[source],
            device_id=(lat, peer), device_id_type=MESH)

    def start1(k, _):
        scatter(k, lax.rem(lon + k, NLON), lon).start()
        return 0

    def wait1(k, _):
        peer = lax.rem(lon + k, NLON)
        scatter(k, peer, peer).wait_recv()
        return 0

    lax.fori_loop(1, NLON, start1, 0)
    first[lon] = part[pl.ds(3 * lon, 3)]
    lax.fori_loop(1, NLON, wait1, 0)
    piece = first[0]
    for n in range(1, NLON):
        piece = piece + first[n]
    second[lat] = piece

    def exchange(k, peer, source):
        return pltpu.make_async_remote_copy(
            src_ref=second.at[lat], dst_ref=second.at[source],
            send_sem=s2.at[k], recv_sem=r2.at[source],
            device_id=(peer, lon), device_id_type=MESH)

    def start2(k, _):
        exchange(k, lax.rem(lat + k, NLAT), lat).start()
        return 0

    def wait2(k, _):
        peer = lax.rem(lat + k, NLAT)
        exchange(k, peer, peer).wait_recv()
        return 0

    lax.fori_loop(1, NLAT, start2, 0)
    lax.fori_loop(1, NLAT, wait2, 0)
    piece = second[0]
    for n in range(1, NLAT):
        piece = piece + second[n]
    whole[pl.ds(3 * lon, 3)] = piece * (1.0 / (512 * 2048))

    def spread(k, peer, source):
        return pltpu.make_async_remote_copy(
            src_ref=whole.at[pl.ds(3 * lon, 3)], dst_ref=whole.at[pl.ds(3 * source, 3)],
            send_sem=s3.at[k], recv_sem=r3.at[source],
            device_id=(lat, peer), device_id_type=MESH)

    def start3(k, _):
        spread(k, lax.rem(lon + k, NLON), lon).start()
        return 0

    def wait3(k, _):
        peer = lax.rem(lon + k, NLON)
        spread(k, peer, peer).wait_recv()
        return 0

    lax.fori_loop(1, NLON, start3, 0)
    lax.fori_loop(1, NLON, wait3, 0)
    out[...] = whole[...]

    def drain(k, _):
        scatter(k, lax.rem(lon + k, NLON), lon).wait_send()
        spread(k, lax.rem(lon + k, NLON), lon).wait_send()
        return 0

    def drain2(k, _):
        exchange(k, lax.rem(lat + k, NLAT), lat).wait_send()
        return 0

    lax.fori_loop(1, NLON, drain, 0)
    lax.fori_loop(1, NLAT, drain2, 0)


def summed(part):
    return pl.pallas_call(
        sum_kernel,
        out_shape=jax.ShapeDtypeStruct((48, 8, 128), F32),
        in_specs=[VM],
        out_specs=VM,
        scratch_shapes=[
            pltpu.VMEM((NLON, 3, 8, 128), F32),
            pltpu.VMEM((NLAT, 3, 8, 128), F32),
            pltpu.VMEM((48, 8, 128), F32),
            pltpu.SemaphoreType.DMA((NLON,)),
            pltpu.SemaphoreType.DMA((NLON,)),
            pltpu.SemaphoreType.DMA((NLAT,)),
            pltpu.SemaphoreType.DMA((NLAT,)),
            pltpu.SemaphoreType.DMA((NLON,)),
            pltpu.SemaphoreType.DMA((NLON,)),
        ],
        compiler_params=pltpu.CompilerParams(collective_id=1, has_side_effects=True),
        name="gradient_sum",
    )(part)


def unpack_kernel(whole, grad1, grad2, gradh, loss):
    packed = jnp.concatenate(
        [jnp.concatenate([whole[6 * g + h] for h in range(6)], axis=1) for g in range(8)], axis=0)
    for t in range(9):
        grad2[t] = packed[:, 64 * t : 64 * (t + 1)]
        grad1[t] = packed[:, 576 + 16 * t : 576 + 16 * t + BANDS]
    gradh[...] = packed[:, 640:768].T[80 : 80 + NCLASS, :]
    loss[...] = packed[0:1, 736:737]


def unpacked(whole):
    return pl.pallas_call(
        unpack_kernel,
        out_shape=(
            jax.ShapeDtypeStruct((9, FEAT, BANDS), F32),
            jax.ShapeDtypeStruct((9, FEAT, FEAT), F32),
            jax.ShapeDtypeStruct((NCLASS, FEAT), F32),
            jax.ShapeDtypeStruct((1, 1), F32),
        ),
        in_specs=[VM],
        out_specs=(VM, VM, VM, VM),
        name="unpack",
    )(whole)


def body(patches, requests, foot, widx, cw, labels, w1, w2, head):
    comp, strip = gather(patches, requests, foot, widx, cw, labels)
    skip, part = tile_pass(comp, strip, w1, w2, head)
    grad1, grad2, gradh, loss = unpacked(summed(part))
    return skip, grad1, grad2, gradh, loss.reshape(())


def solution(mesh):
    placed = (
        P(("lat", "lon"), None),
        P("lat", "lon"),
        P("lat", "lon"),
        P("lat", "lon"),
        P(),
        P("lat", "lon"),
        P(),
        P(),
        P(),
    )
    return jax.shard_map(
        body,
        mesh=mesh,
        in_specs=placed,
        out_specs=(P(None, "lat", "lon"), P(), P(), P(), P()),
        check_vma=False,
    )
```

profile of v0, /device:TPU:1, one launch (start us, length us, event | category | flops | bytes accessed | tf_op | source)
XLA Modules:
  0.0 90.1 jit_solution(17498183973888596038)
XLA Ops:
  0.6 0.0 copy-start
  0.6 1.4 %copy.14.foot = s32[64,8]{1,0:T(8,128)} copy(s32[64,8]{0,1:T(8,128)} %param.11) | data formatting | bytes 4096 | tf_op args[2]
  2.0 1.4 %copy.15.widx = s32[64,8]{1,0:T(8,128)} copy(s32[64,8]{0,1:T(8,128)} %param.12) | data formatting | bytes 4096 | tf_op args[3]
  3.4 0.0 copy-done
  3.4 0.8 copy.16.w1
  4.2 41.3 %gather_blend_halo.1 = (bf16[70,16,128]{2,1,0:T(8,128)(2,1)}, bf16[10,16,128]{2,1,0:T(8,128)(2,1)}) custom-call(bf16[192,1536]{1,0:T(8,128)(2,1)} %patches.1, s32[1,512]{1,0:T(1,128)} %requests.1, s32[64,8]{1,0:T(8,128)} %copy.14.foot, s32[64,8]{1,0:T(8,128)} %copy.15.widx, f32[16]{0:T(128)} %cw.1, s32[64,128]{1,0:T(8,128)} %labels.1), custom_call_target="tpu_custom_call" | custom-call | tf_op jit(solution)/shard_map/gather_blend_halo/pallas_call | solution.py:230
  45.5 21.0 %tile_forward_backward.1 = (bf16[64,64,128]{2,1,0:T(8,128)(2,1)}, f32[48,8,128]{2,1,0:T(8,128)}) custom-call(bf16[70,16,128]{2,1,0:T(8,128)(2,1)} %get-tuple-element.13.comp, bf16[10,16,128]{2,1,0:T(8,128)(2,1)} %get-tuple-element.14.strip, bf16[9,64,12]{2,1,0:T(8,128)(2,1)} %copy.16.w1, bf16[9,64,64]{2,1,0:T(8,128)(2,1)} %w2.1, bf16[11,64]{1,0:T(8,128)(2,1)} %head.1), custom_call_target="tpu_custom_call" | custom-call | tf_op jit(solution)/shard_map/tile_forward_backward/pallas_call | solution.py:430
  66.5 19.9 %gradient_sum.1.whole = f32[48,8,128]{2,1,0:T(8,128)} custom-call(f32[48,8,128]{2,1,0:T(8,128)} %get-tuple-element.16.part), custom_call_target="tpu_custom_call" | custom-call | tf_op jit(solution)/shard_map/gradient_sum/pallas_call | solution.py:555
  86.5 1.9 %unpack.1 = (f32[9,64,12]{2,1,0:T(8,128)}, f32[9,64,64]{2,1,0:T(8,128)}, f32[11,64]{1,0:T(8,128)}, f32[1,1]{1,0:T(1,128)}) custom-call(f32[48,8,128]{2,1,0:T(8,128)} %gradient_sum.1.whole), custom_call_target="tpu_custom_call" | custom-call | tf_op jit(solution)/shard_map/unpack/pallas_call | solution.py:587
  88.3 1.7 %copy.17 = f32[9,64,12]{1,2,0:T(8,128)} copy(f32[9,64,12]{2,1,0:T(8,128)} %get-tuple-element.22) | data formatting | bytes 55296
Async XLA Ops:
  0.6 2.8 %copy-start = (bf16[9,64,12]{1,2,0:T(8,128)(2,1)S(1)}, bf16[9,64,12]{1,2,0:T(8,128)(2,1)}, u32[]{:S(2)}) copy-start(bf16[9,64,12]{1,2,0:T(8,128)(2,1)} %param.15) | copy-start | bytes 41476
where the time goes:
time: 90.7 us; the launch traced here: 90.1 us
  Pallas kernels  84.1 us (93%)
  local copies, waits for them, and re-layouts  5.33 us (6%)
    pallas_call x1, Pallas kernels, gather(): pl.pallas_call(gather_kernel, out_shape=(jax.ShapeDtypeStruct((70, 16, 12...  41.3 us
    pallas_call x1, Pallas kernels, tile_pass(): pl.pallas_call(tile_kernel, out_shape=(jax.ShapeDtypeStruct((FEAT, ROWS,...  21 us
    pallas_call x1, Pallas kernels, summed(): pl.pallas_call(sum_kernel, out_shape=jax.ShapeDtypeStruct((48, 8, 128), F...  19.9 us
    unnamed x6, local copies, waits for them, and re-layouts  5.33 us
    pallas_call x1, Pallas kernels, unpacked(): pl.pallas_call(unpack_kernel, out_shape=(jax.ShapeDtypeStruct((9, FEAT, B...  1.89 us

commit v1 on v0

--- a/solution.py
+++ b/solution.py
@@ -77,11 +77,11 @@
     own = pl.multiple_of((lon // 4) * 128, 128)
     reqs[lon] = requests[:, pl.ds(own, 128)]
 
-    level = widx[...]
+    level = widx[...].astype(F32).T
     weight = jnp.zeros((ROWS, SLOTS), F32)
     for q in range(16):
         weight = jnp.where(level == q, cw[q], weight)
-    entry = foot[...]
+    entry = foot[...].astype(F32).T.astype(jnp.int32)
     weight = jnp.where(entry >= 0, weight, 0.0)
     total = jnp.sum(weight, axis=1, keepdims=True)
     position = lane_iota((ROWS, NLON * BUCKET))
@@ -258,17 +258,17 @@
     )(patches, requests, foot, widx, cw, labels)
 
 
-def sigmoid(v):
-    return 0.5 * jnp.tanh(0.5 * v) + 0.5
-
-
-def slope_of(v, s):
-    return s * (1.0 + v * (1.0 - s))
+def halves(h):
+    return 1.0 + jnp.tanh(h)
+
+
+def twice_slope(h, a):
+    return a * (1.0 + h * (2.0 - a))
 
 
 def tile_kernel(
     comp, strip, w1, w2, head, skip_out, grads,
-    w1k, w2k, w2a, x1, x2, x3, pre1, sk, edge, hid, skip3, acc2, acc1, acch, accl,
+    w1k, w2k, w2a, x1, x2, x3, own, fact1, buf1, buf2, buf3, cols, skip3, acc2, acc1, acch, accl,
 ):
     lat, lon = lax.axis_index("lat"), lax.axis_index("lon")
     has_up, has_down = lat > 0, lat < NLAT - 1
@@ -276,151 +276,164 @@
 
     w1k[...] = jnp.zeros_like(w1k)
     for t in range(9):
-        w1k[:, 16 * t : 16 * t + BANDS] = w1[t]
-        w2k[:, 64 * t : 64 * (t + 1)] = w2[t]
-        w2a[:, 64 * t : 64 * (t + 1)] = w2[8 - t].astype(F32).T.astype(BF16)
+        w1k[:, 16 * t : 16 * t + BANDS] = (w1[t].astype(F32).T * 0.5).astype(BF16)
+        w2k[:, 64 * t : 64 * (t + 1)] = (w2[t].astype(F32) * 0.5).astype(BF16)
+        w2a[:, 64 * t : 64 * (t + 1)] = (0.5 * w2[8 - t].astype(F32).T).astype(BF16)
     headp = jnp.concatenate(
-        [head[...].astype(F32), jnp.zeros((16 - NCLASS, FEAT), F32)], axis=0).astype(BF16)
-
-    def spread(dst, tile, index, tile_f32, left_col, right_col, lane_row, height):
+        [head[...].astype(F32), jnp.zeros((16 - NCLASS, FEAT), F32)], axis=0)
+    head_half = (0.5 * headp).astype(BF16)
+    headp = headp.astype(BF16)
+
+    def spread(dst, tile, index, left_col, right_col, lane_row, height):
         lanes = lane_iota((height, 128))
         put_left = pltpu.roll(left_col, lax.rem(128 - lane_row, 128), 1)
         put_right = pltpu.roll(right_col, lax.rem(255 - lane_row, 128), 1)
-        at = pl.ds(pl.multiple_of(index * 128, 128), 128)
-        dst[0:height, at] = jnp.where(lanes == 0, put_left, pltpu.roll(tile_f32, 1, 1)).astype(BF16)
-        dst[height : 2 * height, at] = tile
-        dst[2 * height : 3 * height, at] = jnp.where(
-            lanes == 127, put_right, pltpu.roll(tile_f32, 127, 1)).astype(BF16)
-
-    comp_left = strip[2].astype(F32)
-    comp_right = strip[7].astype(F32)
+        dst[index, 0:height] = jnp.where(lanes == 0, put_left, pltpu.roll(tile, 1, 1))
+        dst[index, height : 2 * height] = tile
+        dst[index, 2 * height : 3 * height] = jnp.where(
+            lanes == 127, put_right, pltpu.roll(tile, 127, 1))
+
+    def wide(ref, first, count):
+        return jnp.concatenate([ref[first + j] for j in range(count)], axis=1)
+
+    def stack_of(ref, first, count):
+        return jnp.concatenate([wide(ref, first + u, count) for u in (-1, 0, 1)], axis=0)
+
+    comp_left = strip[2]
+    comp_right = strip[7]
 
     def spread_comp(i, _):
         for j in range(7):
             t = i * 7 + j
-            tile = comp[t]
-            spread(x1, tile, t, tile.astype(F32), comp_left, comp_right, t, 16)
+            spread(x1, comp[t], t, comp_left, comp_right, t, 16)
         return 0
 
     lax.fori_loop(0, 10, spread_comp, 0)
 
-    lanes16 = lane_iota((16, 128))
-    del lanes16
-    turned = [[pltpu.roll(strip[s].astype(F32), (128 - u) % 128, 1).astype(BF16) for u in (-1, 0, 1)]
-              for s in range(10)]
+    turned = [[pltpu.roll(strip[s], (128 - u) % 128, 1) for u in (-1, 0, 1)] for s in range(10)]
     lanes64 = lane_iota((FEAT, 128))
     row_ok = ((lanes64 >= 3) | has_up) & ((lanes64 < 67) | has_down) & (lanes64 >= 1) & (lanes64 < 69)
-    for n, s in enumerate((1, 2, 3, 6, 7, 8)):
-        stack = jnp.concatenate([turned[s + v][u] for u in range(3) for v in (-1, 0, 1)], axis=0)
-        pre = dot(w1k[...], stack)
+    beside = (1, 2, 3, 6, 7, 8)
+    half = dot(w1k[...], jnp.concatenate(
+        [jnp.concatenate([turned[s + v][u] for u in range(3) for v in (-1, 0, 1)], axis=0)
+         for s in beside], axis=1))
+    value = half * halves(half)
+    for n, s in enumerate(beside):
         keep = row_ok
         if s in (1, 2):
             keep = keep & has_left
         if s in (7, 8):
             keep = keep & has_right
-        hid[n] = jnp.where(keep, pre * sigmoid(pre), 0.0)
-    hid_left = hid[1]
-    hid_right = hid[4]
-
-    def stack_of(ref, first, count):
-        return jnp.concatenate(
-            [ref[:, pl.ds(pl.multiple_of((first + u) * 128, 128), count * 128)] for u in (-1, 0, 1)],
-            axis=0)
-
-    for first, inside in ((1, has_up), (67, has_down)):
-        pre = dot(w1k[...], stack_of(x1, first, 2))
-        value = jnp.where(inside, pre * sigmoid(pre), 0.0)
-        for j in range(2):
-            tile = value[:, 128 * j : 128 * (j + 1)]
-            spread(x2, tile.astype(BF16), first - 1 + j, tile, hid_left, hid_right, first + j, FEAT)
+        cols[n] = jnp.where(keep, value[:, 128 * n : 128 * (n + 1)], 0.0).astype(BF16)
+
+    half = jnp.concatenate(
+        [dot(w1k[...], stack_of(x1, 1, 2)), dot(w1k[...], stack_of(x1, 67, 2))], axis=1)
+    value = half * halves(half)
+    for j, (index, inside) in enumerate(((0, has_up), (1, has_up), (66, has_down), (67, has_down))):
+        tile = jnp.where(inside, value[:, 128 * j : 128 * (j + 1)], 0.0).astype(BF16)
+        spread(x2, tile, index, cols[1], cols[4], index + 1, FEAT)
+
+    buf1[...] = dot(w1k[...], stack_of(x1, 3, 8))
 
     def conv_one(i, _):
         first = i * 8
-        pre = dot(w1k[...], stack_of(x1, first + 3, 8))
-        pre1[:, pl.ds(pl.multiple_of(first * 128, 128), 1024)] = pre
-        value = pre * sigmoid(pre)
+        left_col, right_col = cols[1], cols[4]
         for j in range(8):
-            tile = value[:, 128 * j : 128 * (j + 1)]
-            spread(x2, tile.astype(BF16), first + 2 + j, tile, hid_left, hid_right, first + 3 + j, FEAT)
+            half = buf1[:, 128 * j : 128 * (j + 1)]
+            a = halves(half)
+            fact1[first + j] = twice_slope(half, a)
+            tile = (half * a).astype(BF16)
+            spread(x2, tile, first + 2 + j, left_col, right_col, first + 3 + j, FEAT)
+        buf1[...] = dot(w1k[...], stack_of(x1, jnp.minimum(first + 11, 59), 8))
         return 0
 
     lax.fori_loop(0, 8, conv_one, 0)
 
-    def head_of(pre, label):
-        width = pre.shape[1]
-        s = sigmoid(pre)
-        skip = (pre * s).astype(BF16)
-        logits = dot(headp, skip)
+    def head_of(half, label):
+        width = half.shape[1]
+        a = halves(half)
+        skip = half * a
+        skip_bf16 = skip.astype(BF16)
+        logits = dot(headp, skip_bf16)
         classes = lax.broadcasted_iota(jnp.int32, (16, width), 0)
         power = jnp.where(classes < NCLASS, jnp.exp(logits), 0.0)
         total = jnp.sum(power, axis=0, keepdims=True)
         onehot = classes == label.astype(jnp.int32)
-        error = (power / total - jnp.where(onehot, 1.0, 0.0)).astype(BF16)
-        slope = dot_tn(headp, error) * slope_of(pre, s)
+        error = (power * (1.0 / total) - jnp.where(onehot, 1.0, 0.0)).astype(BF16)
+        slope = dot_tn(head_half, error) * twice_slope(half, a)
         loss = jnp.log(total) - jnp.sum(jnp.where(onehot, logits, 0.0), axis=0, keepdims=True)
-        return skip, error, slope, loss
-
-    edge[:, 0:128] = dot(w2k[...], stack_of(x2, 1, 1))
-    edge[:, 128:256] = dot(w2k[...], stack_of(x2, 66, 1))
-    for n, middle in enumerate((1, 4)):
-        stack = jnp.concatenate(
-            [pltpu.roll(hid[middle + v], (128 - u) % 128, 1).astype(BF16)
-             for u in (-1, 0, 1) for v in (-1, 0, 1)], axis=0)
-        edge[:, 256 + 128 * n : 384 + 128 * n] = dot(w2k[...], stack)
+        return skip, skip_bf16, error, slope, loss
 
     def label_row(tile):
         return tile.astype(F32)[BANDS : BANDS + 1, :]
 
+    beside = [jnp.concatenate(
+        [pltpu.roll(cols[middle + v], (128 - u) % 128, 1) for u in (-1, 0, 1) for v in (-1, 0, 1)],
+        axis=0) for middle in (1, 4)]
+    around = jnp.concatenate([stack_of(x2, 1, 1), stack_of(x2, 66, 1)] + beside, axis=1)
     edge_label = jnp.concatenate(
         [label_row(comp[2]), label_row(comp[67]), label_row(strip[2]), label_row(strip[7])], axis=1)
-    _, _, edge_slope, _ = head_of(edge[...], edge_label)
-    slope_left = jnp.where(row_ok & has_left, edge_slope[:, 256:384], 0.0)
-    slope_right = jnp.where(row_ok & has_right, edge_slope[:, 384:512], 0.0)
-    slope_top = jnp.where(has_up, edge_slope[:, 0:128], 0.0)
-    slope_bottom = jnp.where(has_down, edge_slope[:, 128:256], 0.0)
-    hid[0] = slope_left
-    hid[2] = slope_right
-    spread(x3, slope_top.astype(BF16), 0, slope_top, slope_left, slope_right, 2, FEAT)
-    spread(x3, slope_bottom.astype(BF16), 65, slope_bottom, slope_left, slope_right, 67, FEAT)
-
-    acc2[...] = jnp.zeros_like(acc2)
+    _, _, _, edge_slope, _ = head_of(dot(w2k[...], around), edge_label)
+    slope_left = jnp.where(row_ok & has_left, edge_slope[:, 256:384], 0.0).astype(BF16)
+    slope_right = jnp.where(row_ok & has_right, edge_slope[:, 384:512], 0.0).astype(BF16)
+    slope_top = jnp.where(has_up, edge_slope[:, 0:128], 0.0).astype(BF16)
+    slope_bottom = jnp.where(has_down, edge_slope[:, 128:256], 0.0).astype(BF16)
+    cols[0] = slope_left
+    cols[2] = slope_right
+    spread(x3, slope_top, 0, slope_left, slope_right, 2, FEAT)
+    spread(x3, slope_bottom, 65, slope_left, slope_right, 67, FEAT)
+    for index in (0, 1, 66, 67):
+        own[index] = jnp.zeros((FEAT, 128), BF16)
+
     acc1[...] = jnp.zeros_like(acc1)
     acch[...] = jnp.zeros_like(acch)
     accl[...] = jnp.zeros_like(accl)
+    buf2[...] = dot(w2k[...], stack_of(x2, 2, 8))
 
     def conv_two(i, _):
         first = i * 8
-        stack = stack_of(x2, first + 2, 8)
-        pre = dot(w2k[...], stack)
-        label = jnp.concatenate([label_row(comp[first + 3 + j]) for j in range(8)], axis=1)
-        skip, error, slope, loss = head_of(pre, label)
-        acch[...] += dot_nt(skip, error)
-        accl[...] += loss
-        skip_f32 = skip.astype(F32)
-        left_col, right_col = hid[0], hid[2]
-        for j in range(8):
-            tile = slope[:, 128 * j : 128 * (j + 1)]
-            spread(x3, tile.astype(BF16), first + 1 + j, tile, left_col, right_col, first + 3 + j, FEAT)
-            skip3[:, j, :] = skip_f32[:, 128 * j : 128 * (j + 1)]
+        left_col, right_col = cols[0], cols[2]
+        heads = []
+        for j in range(0, 8, 2):
+            label = jnp.concatenate([label_row(comp[first + 3 + j + m]) for m in range(2)], axis=1)
+            skip, skip_bf16, error, slope, loss = head_of(buf2[:, 128 * j : 128 * (j + 2)], label)
+            heads.append((skip_bf16, error))
+            accl[...] += loss
+            for m in range(2):
+                tile = slope[:, 128 * m : 128 * (m + 1)].astype(BF16)
+                spread(x3, tile, first + 1 + j + m, left_col, right_col, first + 3 + j + m, FEAT)
+                own[first + 2 + j + m] = tile
+                skip3[:, j + m, :] = skip[:, 128 * m : 128 * (m + 1)]
+        acch[...] += dot_nt(jnp.concatenate([h[0] for h in heads], axis=1),
+                            jnp.concatenate([h[1] for h in heads], axis=1))
         skip_out[:, pl.ds(pl.multiple_of(first, 8), 8), :] = skip3[...].astype(BF16)
-        acc2[...] += dot_nt(slope.astype(BF16), stack)
+        buf2[...] = dot(w2k[...], stack_of(x2, jnp.minimum(first + 10, 58), 8))
         return 0
 
     lax.fori_loop(0, 8, conv_two, 0)
+
+    def grad_two(first, count):
+        lhs = jnp.concatenate([wide(own, first - u, count) for u in (-1, 0, 1)], axis=0)
+        return dot_nt(lhs, wide(x2, first, count))
+
+    acc2[...] = grad_two(1, 1) + grad_two(66, 1)
+    buf3[...] = dot(w2a[...], stack_of(x3, 1, 8))
 
     def back_one(i, _):
         first = i * 8
-        back = dot(w2a[...], stack_of(x3, first + 1, 8))
-        pre = pre1[:, pl.ds(pl.multiple_of(first * 128, 128), 1024)]
-        slope = (back * slope_of(pre, sigmoid(pre))).astype(BF16)
-        acc1[...] += dot_nt(slope, stack_of(x1, first + 3, 8))
+        slopes = [(buf3[:, 128 * j : 128 * (j + 1)] * fact1[first + j]).astype(BF16)
+                  for j in range(8)]
+        acc1[...] += dot_nt(jnp.concatenate(slopes, axis=1), stack_of(x1, first + 3, 8))
+        acc2[...] += grad_two(first + 2, 8)
+        buf3[...] = dot(w2a[...], stack_of(x3, jnp.minimum(first + 9, 57), 8))
         return 0
 
     lax.fori_loop(0, 8, back_one, 0)
 
     loss_total = jnp.sum(jnp.sum(accl[...], axis=1, keepdims=True), axis=0, keepdims=True)
     packed = jnp.concatenate(
-        [acc2[...], acc1[...], acch[...], jnp.broadcast_to(loss_total, (FEAT, 32))], axis=1)
+        [acc2[64 * u : 64 * (u + 1), :] for u in range(3)]
+        + [acc1[...], acch[...], jnp.broadcast_to(loss_total, (FEAT, 32))], axis=1)
     for g in range(8):
         for h in range(6):
             grads[6 * g + h] = packed[8 * g : 8 * (g + 1), 128 * h : 128 * (h + 1)]
@@ -439,18 +452,20 @@
             pltpu.VMEM((64, 144), BF16),
             pltpu.VMEM((64, 576), BF16),
             pltpu.VMEM((64, 576), BF16),
-            pltpu.VMEM((48, 70 * 128), BF16),
-            pltpu.VMEM((192, 68 * 128), BF16),
-            pltpu.VMEM((192, 66 * 128), BF16),
-            pltpu.VMEM((64, 64 * 128), F32),
-            pltpu.VMEM((8, 128), F32),
-            pltpu.VMEM((64, 512), F32),
-            pltpu.VMEM((6, 64, 128), F32),
+            pltpu.VMEM((70, 48, 128), BF16),
+            pltpu.VMEM((68, 192, 128), BF16),
+            pltpu.VMEM((66, 192, 128), BF16),
+            pltpu.VMEM((68, 64, 128), BF16),
+            pltpu.VMEM((64, 64, 128), F32),
+            pltpu.VMEM((64, 1024), F32),
+            pltpu.VMEM((64, 1024), F32),
+            pltpu.VMEM((64, 1024), F32),
+            pltpu.VMEM((6, 64, 128), BF16),
             pltpu.VMEM((64, 8, 128), F32),
-            pltpu.VMEM((64, 576), F32),
+            pltpu.VMEM((192, 192), F32),
             pltpu.VMEM((64, 144), F32),
             pltpu.VMEM((64, 16), F32),
-            pltpu.VMEM((1, 1024), F32),
+            pltpu.VMEM((1, 256), F32),
         ],
         name="tile_forward_backward",
     )(comp, strip, w1, w2, head)
@@ -576,10 +591,11 @@
 def unpack_kernel(whole, grad1, grad2, gradh, loss):
     packed = jnp.concatenate(
         [jnp.concatenate([whole[6 * g + h] for h in range(6)], axis=1) for g in range(8)], axis=0)
+    packed_t = packed.T
     for t in range(9):
         grad2[t] = packed[:, 64 * t : 64 * (t + 1)]
-        grad1[t] = packed[:, 576 + 16 * t : 576 + 16 * t + BANDS]
-    gradh[...] = packed[:, 640:768].T[80 : 80 + NCLASS, :]
+        grad1[t] = packed_t[576 + 16 * t : 576 + 16 * t + BANDS, :]
+    gradh[...] = packed_t[720 : 720 + NCLASS, :]
     loss[...] = packed[0:1, 736:737]
 
 
@@ -587,7 +603,7 @@
     return pl.pallas_call(
         unpack_kernel,
         out_shape=(
-            jax.ShapeDtypeStruct((9, FEAT, BANDS), F32),
+            jax.ShapeDtypeStruct((9, BANDS, FEAT), F32),
             jax.ShapeDtypeStruct((9, FEAT, FEAT), F32),
             jax.ShapeDtypeStruct((NCLASS, FEAT), F32),
             jax.ShapeDtypeStruct((1, 1), F32),
@@ -599,10 +615,10 @@
 
 
 def body(patches, requests, foot, widx, cw, labels, w1, w2, head):
-    comp, strip = gather(patches, requests, foot, widx, cw, labels)
-    skip, part = tile_pass(comp, strip, w1, w2, head)
+    comp, strip = gather(patches, requests, foot.T, widx.T, cw, labels)
+    skip, part = tile_pass(comp, strip, jnp.swapaxes(w1, 1, 2), w2, head)
     grad1, grad2, gradh, loss = unpacked(summed(part))
-    return skip, grad1, grad2, gradh, loss.reshape(())
+    return skip, jnp.swapaxes(grad1, 1, 2), grad2, gradh, loss.reshape(())
 
 
 def solution(mesh):

time: 90.7 us -> 81.8 us (0.902)
  local copies, waits for them, and re-layouts: 5.33 us -> 0 us
  Pallas kernels: 84.1 us -> 80.7 us
    unnamed x6 -> x0, local copies, waits for them, and re-layouts: 5.33 us -> none
    pallas_call x1, Pallas kernels: 21 us -> 17.6 us  [tile_pass(): pl.pallas_call(tile_kernel, out_shape=(jax.ShapeDtypeStruct((FEAT, ROWS,...]
where the time goes in v1:
time: 81.8 us; the launch traced here: 81.4 us
  Pallas kernels  80.7 us (99%)
    pallas_call x1, Pallas kernels, gather(): pl.pallas_call(gather_kernel, out_shape=(jax.ShapeDtypeStruct((70, 16, 12...  41.4 us
    pallas_call x1, Pallas kernels, summed(): pl.pallas_call(sum_kernel, out_shape=jax.ShapeDtypeStruct((48, 8, 128), F...  19.9 us
    pallas_call x1, Pallas kernels, tile_pass(): pl.pallas_call(tile_kernel, out_shape=(jax.ShapeDtypeStruct((FEAT, ROWS,...  17.6 us
    pallas_call x1, Pallas kernels, unpacked(): pl.pallas_call(unpack_kernel, out_shape=(jax.ShapeDtypeStruct((9, BANDS,...  1.79 us

profile of v1, /device:TPU:1, one launch (start us, length us, event | category | flops | bytes accessed | tf_op | source)
XLA Modules:
  0.0 81.4 jit_solution(2247007407332909368)
XLA Ops:
  0.6 41.4 %gather_blend_halo.1 = (bf16[70,16,128]{2,1,0:T(8,128)(2,1)}, bf16[10,16,128]{2,1,0:T(8,128)(2,1)}) custom-call(bf16[192,1536]{1,0:T(8,128)(2,1)} %patches.1, s32[1,512]{1,0:T(1,128)} %requests.1, s32[8,64]{1,0:T(8,128)} %bitcast.6, s32[8,64]{1,0:T(8,128)} %bitcast.7, f32[16]{0:T(128)} %cw.1, s32[64,128]{1,0:T(8,128)} %labels.1), custom_call_target="tpu_custom_call" | custom-call | tf_op jit(solution)/shard_map/gather_blend_halo/pallas_call | solution.py:230
  42.0 17.6 %tile_forward_backward.1 = (bf16[64,64,128]{2,1,0:T(8,128)(2,1)}, f32[48,8,128]{2,1,0:T(8,128)}) custom-call(bf16[70,16,128]{2,1,0:T(8,128)(2,1)} %get-tuple-element.13.comp, bf16[10,16,128]{2,1,0:T(8,128)(2,1)} %get-tuple-element.14.strip, bf16[9,12,64]{2,1,0:T(8,128)(2,1)} %bitcast.5, bf16[9,64,64]{2,1,0:T(8,128)(2,1)} %w2.1, bf16[11,64]{1,0:T(8,128)(2,1)} %head.1), custom_call_target="tpu_custom_call" | custom-call | tf_op jit(solution)/shard_map/tile_forward_backward/pallas_call | solution.py:443
  59.6 19.9 %gradient_sum.1.whole = f32[48,8,128]{2,1,0:T(8,128)} custom-call(f32[48,8,128]{2,1,0:T(8,128)} %get-tuple-element.16.part), custom_call_target="tpu_custom_call" | custom-call | tf_op jit(solution)/shard_map/gradient_sum/pallas_call | solution.py:570
  79.6 1.8 %unpack.1 = (f32[9,12,64]{2,1,0:T(8,128)}, f32[9,64,64]{2,1,0:T(8,128)}, f32[11,64]{1,0:T(8,128)}, f32[1,1]{1,0:T(1,128)}) custom-call(f32[48,8,128]{2,1,0:T(8,128)} %gradient_sum.1.whole), custom_call_target="tpu_custom_call" | custom-call | tf_op jit(solution)/shard_map/unpack/pallas_call | solution.py:603

commit v2 on v1

--- a/solution.py
+++ b/solution.py
@@ -156,9 +156,17 @@
     for x in range(3):
         hsend[3 + x] = picked[:, x, :].astype(BF16)
         hsend[6 + x] = picked[:, 3 + x, :].astype(BF16)
-    for r in range(3):
-        hsend[r] = bands[:, r, :].astype(BF16)
-        hsend[9 + r] = bands[:, ROWS - 3 + r, :].astype(BF16)
+    swap_out = lax.broadcasted_iota(jnp.int32, (128, 128), 0)
+    swap = jnp.where((swap_out % 16) * 8 + swap_out // 16 == lane_iota((128, 128)), 1.0, 0.0)
+    swap = swap.astype(BF16)
+
+    def row_tiles(g):
+        block = bands[:, 8 * g : 8 * g + 8, :].reshape(128, COLS).astype(BF16)
+        return dot(swap, block).astype(BF16).reshape(8, 16, COLS)
+
+    top, bottom = row_tiles(0), row_tiles(7)
+    hsend[0:3] = top[0:3]
+    hsend[9:12] = bottom[5:8]
 
     def halo_copies():
         made = [
@@ -182,8 +190,10 @@
     for copy in copies:
         copy.start()
 
-    for r in range(ROWS):
-        comp[3 + r] = bands[:, r, :].astype(BF16)
+    comp[3:11] = top
+    for g in range(1, 7):
+        comp[3 + 8 * g : 11 + 8 * g] = row_tiles(g)
+    comp[59:67] = bottom
 
     for copy in copies:
         copy.wait_recv()
@@ -267,10 +277,26 @@
 
 
 def tile_kernel(
-    comp, strip, w1, w2, head, skip_out, grads,
-    w1k, w2k, w2a, x1, x2, x3, own, fact1, buf1, buf2, buf3, cols, skip3, acc2, acc1, acch, accl,
+    comp, strip, w1, w2, head, skip_out, out_a, out_b,
+    w1k, w2k, w2a, x1, x2, x3, fact1, buf1, buf2, buf3, cols, acc2, acc1, acch, accl,
+    part_a, part_b, lat_a, lat_b, lon_a, lon_b, all_a, all_b,
+    s1a, r1a, s1b, r1b, s2a, r2a, s2b, r2b, s3a, r3a, s3b, r3b,
 ):
     lat, lon = lax.axis_index("lat"), lax.axis_index("lon")
+    barrier = pltpu.get_barrier_semaphore()
+
+    def greet_lon(k, _):
+        pl.semaphore_signal(
+            barrier, inc=1, device_id=(lat, lax.rem(lon + k, NLON)), device_id_type=MESH)
+        return 0
+
+    def greet_lat(k, _):
+        pl.semaphore_signal(
+            barrier, inc=1, device_id=(lax.rem(lat + k, NLAT), lon), device_id_type=MESH)
+        return 0
+
+    lax.fori_loop(1, NLON, greet_lon, 0)
+    lax.fori_loop(1, NLAT, greet_lat, 0)
     has_up, has_down = lat > 0, lat < NLAT - 1
     has_left, has_right = lon > 0, lon < NLON - 1
 
@@ -352,9 +378,8 @@
     def head_of(half, label):
         width = half.shape[1]
         a = halves(half)
-        skip = half * a
-        skip_bf16 = skip.astype(BF16)
-        logits = dot(headp, skip_bf16)
+        skip = (half * a).astype(BF16)
+        logits = dot(headp, skip)
         classes = lax.broadcasted_iota(jnp.int32, (16, width), 0)
         power = jnp.where(classes < NCLASS, jnp.exp(logits), 0.0)
         total = jnp.sum(power, axis=0, keepdims=True)
@@ -362,7 +387,7 @@
         error = (power * (1.0 / total) - jnp.where(onehot, 1.0, 0.0)).astype(BF16)
         slope = dot_tn(head_half, error) * twice_slope(half, a)
         loss = jnp.log(total) - jnp.sum(jnp.where(onehot, logits, 0.0), axis=0, keepdims=True)
-        return skip, skip_bf16, error, slope, loss
+        return skip, error, slope, loss
 
     def label_row(tile):
         return tile.astype(F32)[BANDS : BANDS + 1, :]
@@ -373,7 +398,7 @@
     around = jnp.concatenate([stack_of(x2, 1, 1), stack_of(x2, 66, 1)] + beside, axis=1)
     edge_label = jnp.concatenate(
         [label_row(comp[2]), label_row(comp[67]), label_row(strip[2]), label_row(strip[7])], axis=1)
-    _, _, _, edge_slope, _ = head_of(dot(w2k[...], around), edge_label)
+    _, _, edge_slope, _ = head_of(dot(w2k[...], around), edge_label)
     slope_left = jnp.where(row_ok & has_left, edge_slope[:, 256:384], 0.0).astype(BF16)
     slope_right = jnp.where(row_ok & has_right, edge_slope[:, 384:512], 0.0).astype(BF16)
     slope_top = jnp.where(has_up, edge_slope[:, 0:128], 0.0).astype(BF16)
@@ -382,9 +407,11 @@
     cols[2] = slope_right
     spread(x3, slope_top, 0, slope_left, slope_right, 2, FEAT)
     spread(x3, slope_bottom, 65, slope_left, slope_right, 67, FEAT)
-    for index in (0, 1, 66, 67):
-        own[index] = jnp.zeros((FEAT, 128), BF16)
-
+
+    swap_out = lax.broadcasted_iota(jnp.int32, (128, 128), 0)
+    swap = jnp.where((swap_out % 8) * 16 + swap_out // 8 == lane_iota((128, 128)), 1.0, 0.0)
+    swap = swap.astype(BF16)
+    acc2[...] = jnp.zeros_like(acc2)
     acc1[...] = jnp.zeros_like(acc1)
     acch[...] = jnp.zeros_like(acch)
     accl[...] = jnp.zeros_like(accl)
@@ -393,30 +420,65 @@
     def conv_two(i, _):
         first = i * 8
         left_col, right_col = cols[0], cols[2]
-        heads = []
+        heads, slopes = [], []
         for j in range(0, 8, 2):
             label = jnp.concatenate([label_row(comp[first + 3 + j + m]) for m in range(2)], axis=1)
-            skip, skip_bf16, error, slope, loss = head_of(buf2[:, 128 * j : 128 * (j + 2)], label)
-            heads.append((skip_bf16, error))
+            skip, error, slope, loss = head_of(buf2[:, 128 * j : 128 * (j + 2)], label)
+            heads.append((skip, error))
             accl[...] += loss
             for m in range(2):
                 tile = slope[:, 128 * m : 128 * (m + 1)].astype(BF16)
                 spread(x3, tile, first + 1 + j + m, left_col, right_col, first + 3 + j + m, FEAT)
-                own[first + 2 + j + m] = tile
-                skip3[:, j + m, :] = skip[:, 128 * m : 128 * (m + 1)]
+                slopes.append(tile)
         acch[...] += dot_nt(jnp.concatenate([h[0] for h in heads], axis=1),
                             jnp.concatenate([h[1] for h in heads], axis=1))
-        skip_out[:, pl.ds(pl.multiple_of(first, 8), 8), :] = skip3[...].astype(BF16)
+        rows = [heads[j // 2][0][:, 128 * (j % 2) : 128 * (j % 2 + 1)] for j in range(8)]
+        block = jnp.concatenate(
+            [jnp.concatenate([row[16 * g : 16 * (g + 1)] for g in range(4)], axis=1) for row in rows],
+            axis=0)
+        block = dot(swap, block).astype(BF16)
+        for g in range(4):
+            skip_out[16 * g : 16 * (g + 1), pl.ds(pl.multiple_of(first, 8), 8), :] = (
+                block[:, 128 * g : 128 * (g + 1)].reshape(16, 8, 128))
+        acc2[...] += dot_nt(jnp.concatenate(slopes, axis=1), stack_of(x2, first + 2, 8))
         buf2[...] = dot(w2k[...], stack_of(x2, jnp.minimum(first + 10, 58), 8))
         return 0
 
     lax.fori_loop(0, 8, conv_two, 0)
 
-    def grad_two(first, count):
-        lhs = jnp.concatenate([wide(own, first - u, count) for u in (-1, 0, 1)], axis=0)
-        return dot_nt(lhs, wide(x2, first, count))
-
-    acc2[...] = grad_two(1, 1) + grad_two(66, 1)
+    loss_total = jnp.sum(jnp.sum(accl[...], axis=1, keepdims=True), axis=0, keepdims=True)
+    packed = jnp.concatenate(
+        [acc2[...], acch[...], jnp.broadcast_to(loss_total, (FEAT, 48))], axis=1)
+    for g in range(NLAT):
+        part_a[g] = packed[8 * g : 8 * (g + 1), :]
+    pl.semaphore_wait(barrier, NLON - 1 + NLAT - 1)
+
+    def over_lat(k, part, land, send, recv, source):
+        peer = lax.rem(lat + k, NLAT)
+        return pltpu.make_async_remote_copy(
+            src_ref=part.at[peer], dst_ref=land.at[source], send_sem=send.at[k],
+            recv_sem=recv.at[source], device_id=(peer, lon), device_id_type=MESH)
+
+    def over_lon(k, land, send, recv, source):
+        return pltpu.make_async_remote_copy(
+            src_ref=land.at[lon], dst_ref=land.at[source], send_sem=send.at[k],
+            recv_sem=recv.at[source], device_id=(lat, lax.rem(lon + k, NLON)), device_id_type=MESH)
+
+    def back_lat(k, land, send, recv, source):
+        return pltpu.make_async_remote_copy(
+            src_ref=land.at[lat], dst_ref=land.at[source], send_sem=send.at[k],
+            recv_sem=recv.at[source], device_id=(lax.rem(lat + k, NLAT), lon), device_id_type=MESH)
+
+    def each(count, do):
+        def step(k, _):
+            do(k)
+            return 0
+
+        lax.fori_loop(1, count, step, 0)
+
+    each(NLAT, lambda k: over_lat(k, part_a, lat_a, s1a, r1a, lat).start())
+    lat_a[lat] = part_a[lat]
+
     buf3[...] = dot(w2a[...], stack_of(x3, 1, 8))
 
     def back_one(i, _):
@@ -424,19 +486,58 @@
         slopes = [(buf3[:, 128 * j : 128 * (j + 1)] * fact1[first + j]).astype(BF16)
                   for j in range(8)]
         acc1[...] += dot_nt(jnp.concatenate(slopes, axis=1), stack_of(x1, first + 3, 8))
-        acc2[...] += grad_two(first + 2, 8)
         buf3[...] = dot(w2a[...], stack_of(x3, jnp.minimum(first + 9, 57), 8))
         return 0
 
     lax.fori_loop(0, 8, back_one, 0)
 
-    loss_total = jnp.sum(jnp.sum(accl[...], axis=1, keepdims=True), axis=0, keepdims=True)
-    packed = jnp.concatenate(
-        [acc2[64 * u : 64 * (u + 1), :] for u in range(3)]
-        + [acc1[...], acch[...], jnp.broadcast_to(loss_total, (FEAT, 32))], axis=1)
-    for g in range(8):
-        for h in range(6):
-            grads[6 * g + h] = packed[8 * g : 8 * (g + 1), 128 * h : 128 * (h + 1)]
+    packed = jnp.concatenate([acc1[...], jnp.zeros((FEAT, 112), F32)], axis=1)
+    for g in range(NLAT):
+        part_b[g] = packed[8 * g : 8 * (g + 1), :]
+    each(NLAT, lambda k: over_lat(k, part_b, lat_b, s1b, r1b, lat).start())
+    lat_b[lat] = part_b[lat]
+
+    def added(ref, count):
+        result = ref[0]
+        for n in range(1, count):
+            result = result + ref[n]
+        return result
+
+    def lat_source(k):
+        return lax.rem(lat + k, NLAT)
+
+    def lon_source(k):
+        return lax.rem(lon + k, NLON)
+
+    each(NLAT, lambda k: over_lat(k, part_a, lat_a, s1a, r1a, lat_source(k)).wait_recv())
+    lon_a[lon] = added(lat_a, NLAT)
+    each(NLON, lambda k: over_lon(k, lon_a, s2a, r2a, lon).start())
+    each(NLAT, lambda k: over_lat(k, part_b, lat_b, s1b, r1b, lat_source(k)).wait_recv())
+    lon_b[lon] = added(lat_b, NLAT)
+    each(NLON, lambda k: over_lon(k, lon_b, s2b, r2b, lon).start())
+    each(NLON, lambda k: over_lon(k, lon_a, s2a, r2a, lon_source(k)).wait_recv())
+    all_a[lat] = added(lon_a, NLON) * (1.0 / (512 * 2048))
+    each(NLAT, lambda k: back_lat(k, all_a, s3a, r3a, lat).start())
+    each(NLON, lambda k: over_lon(k, lon_b, s2b, r2b, lon_source(k)).wait_recv())
+    all_b[lat] = added(lon_b, NLON) * (1.0 / (512 * 2048))
+    each(NLAT, lambda k: back_lat(k, all_b, s3b, r3b, lat).start())
+    each(NLAT, lambda k: back_lat(k, all_a, s3a, r3a, lat_source(k)).wait_recv())
+    out_a[...] = all_a[...]
+    each(NLAT, lambda k: back_lat(k, all_b, s3b, r3b, lat_source(k)).wait_recv())
+    out_b[...] = all_b[...]
+
+    def drain_lat(k):
+        over_lat(k, part_a, lat_a, s1a, r1a, lat).wait_send()
+        over_lat(k, part_b, lat_b, s1b, r1b, lat).wait_send()
+        back_lat(k, all_a, s3a, r3a, lat).wait_send()
+        back_lat(k, all_b, s3b, r3b, lat).wait_send()
+
+    def drain_lon(k):
+        over_lon(k, lon_a, s2a, r2a, lon).wait_send()
+        over_lon(k, lon_b, s2b, r2b, lon).wait_send()
+
+    each(NLAT, drain_lat)
+    each(NLON, drain_lon)
 
 
 def tile_pass(comp, strip, w1, w2, head):
@@ -444,10 +545,11 @@
         tile_kernel,
         out_shape=(
             jax.ShapeDtypeStruct((FEAT, ROWS, COLS), BF16),
-            jax.ShapeDtypeStruct((48, 8, 128), F32),
+            jax.ShapeDtypeStruct((NLAT, 8, 640), F32),
+            jax.ShapeDtypeStruct((NLAT, 8, 256), F32),
         ),
         in_specs=[VM] * 5,
-        out_specs=(VM, VM),
+        out_specs=(VM, VM, VM),
         scratch_shapes=[
             pltpu.VMEM((64, 144), BF16),
             pltpu.VMEM((64, 576), BF16),
@@ -455,151 +557,43 @@
             pltpu.VMEM((70, 48, 128), BF16),
             pltpu.VMEM((68, 192, 128), BF16),
             pltpu.VMEM((66, 192, 128), BF16),
-            pltpu.VMEM((68, 64, 128), BF16),
             pltpu.VMEM((64, 64, 128), F32),
             pltpu.VMEM((64, 1024), F32),
             pltpu.VMEM((64, 1024), F32),
             pltpu.VMEM((64, 1024), F32),
             pltpu.VMEM((6, 64, 128), BF16),
-            pltpu.VMEM((64, 8, 128), F32),
-            pltpu.VMEM((192, 192), F32),
+            pltpu.VMEM((64, 576), F32),
             pltpu.VMEM((64, 144), F32),
             pltpu.VMEM((64, 16), F32),
             pltpu.VMEM((1, 256), F32),
-        ],
-        name="tile_forward_backward",
+            pltpu.VMEM((NLAT, 8, 640), F32),
+            pltpu.VMEM((NLAT, 8, 256), F32),
+            pltpu.VMEM((NLAT, 8, 640), F32),
+            pltpu.VMEM((NLAT, 8, 256), F32),
+            pltpu.VMEM((NLON, 8, 640), F32),
+            pltpu.VMEM((NLON, 8, 256), F32),
+            pltpu.VMEM((NLAT, 8, 640), F32),
+            pltpu.VMEM((NLAT, 8, 256), F32),
+        ]
+        + [pltpu.SemaphoreType.DMA((NLAT,))] * 4
+        + [pltpu.SemaphoreType.DMA((NLON,))] * 4
+        + [pltpu.SemaphoreType.DMA((NLAT,))] * 4,
+        compiler_params=pltpu.CompilerParams(collective_id=1, has_side_effects=True),
+        name="tile_forward_backward_sum",
     )(comp, strip, w1, w2, head)
 
 
-def sum_kernel(part, out, first, second, whole, s1, r1, s2, r2, s3, r3):
-    lat, lon = lax.axis_index("lat"), lax.axis_index("lon")
-    barrier = pltpu.get_barrier_semaphore()
-
-    def greet_lon(k, _):
-        pl.semaphore_signal(
-            barrier, inc=1, device_id=(lat, lax.rem(lon + k, NLON)), device_id_type=MESH)
-        return 0
-
-    def greet_lat(k, _):
-        pl.semaphore_signal(
-            barrier, inc=1, device_id=(lax.rem(lat + k, NLAT), lon), device_id_type=MESH)
-        return 0
-
-    lax.fori_loop(1, NLON, greet_lon, 0)
-    lax.fori_loop(1, NLAT, greet_lat, 0)
-    pl.semaphore_wait(barrier, NLON - 1 + NLAT - 1)
-
-    def scatter(k, peer, source):
-        return pltpu.make_async_remote_copy(
-            src_ref=part.at[pl.ds(3 * peer, 3)], dst_ref=first.at[source],
-            send_sem=s1.at[k], recv_sem=r1.at[source],
-            device_id=(lat, peer), device_id_type=MESH)
-
-    def start1(k, _):
-        scatter(k, lax.rem(lon + k, NLON), lon).start()
-        return 0
-
-    def wait1(k, _):
-        peer = lax.rem(lon + k, NLON)
-        scatter(k, peer, peer).wait_recv()
-        return 0
-
-    lax.fori_loop(1, NLON, start1, 0)
-    first[lon] = part[pl.ds(3 * lon, 3)]
-    lax.fori_loop(1, NLON, wait1, 0)
-    piece = first[0]
-    for n in range(1, NLON):
-        piece = piece + first[n]
-    second[lat] = piece
-
-    def exchange(k, peer, source):
-        return pltpu.make_async_remote_copy(
-            src_ref=second.at[lat], dst_ref=second.at[source],
-            send_sem=s2.at[k], recv_sem=r2.at[source],
-            device_id=(peer, lon), device_id_type=MESH)
-
-    def start2(k, _):
-        exchange(k, lax.rem(lat + k, NLAT), lat).start()
-        return 0
-
-    def wait2(k, _):
-        peer = lax.rem(lat + k, NLAT)
-        exchange(k, peer, peer).wait_recv()
-        return 0
-
-    lax.fori_loop(1, NLAT, start2, 0)
-    lax.fori_loop(1, NLAT, wait2, 0)
-    piece = second[0]
-    for n in range(1, NLAT):
-        piece = piece + second[n]
-    whole[pl.ds(3 * lon, 3)] = piece * (1.0 / (512 * 2048))
-
-    def spread(k, peer, source):
-        return pltpu.make_async_remote_copy(
-            src_ref=whole.at[pl.ds(3 * lon, 3)], dst_ref=whole.at[pl.ds(3 * source, 3)],
-            send_sem=s3.at[k], recv_sem=r3.at[source],
-            device_id=(lat, peer), device_id_type=MESH)
-
-    def start3(k, _):
-        spread(k, lax.rem(lon + k, NLON), lon).start()
-        return 0
-
-    def wait3(k, _):
-        peer = lax.rem(lon + k, NLON)
-        spread(k, peer, peer).wait_recv()
-        return 0
-
-    lax.fori_loop(1, NLON, start3, 0)
-    lax.fori_loop(1, NLON, wait3, 0)
-    out[...] = whole[...]
-
-    def drain(k, _):
-        scatter(k, lax.rem(lon + k, NLON), lon).wait_send()
-        spread(k, lax.rem(lon + k, NLON), lon).wait_send()
-        return 0
-
-    def drain2(k, _):
-        exchange(k, lax.rem(lat + k, NLAT), lat).wait_send()
-        return 0
-
-    lax.fori_loop(1, NLON, drain, 0)
-    lax.fori_loop(1, NLAT, drain2, 0)
-
-
-def summed(part):
-    return pl.pallas_call(
-        sum_kernel,
-        out_shape=jax.ShapeDtypeStruct((48, 8, 128), F32),
-        in_specs=[VM],
-        out_specs=VM,
-        scratch_shapes=[
-            pltpu.VMEM((NLON, 3, 8, 128), F32),
-            pltpu.VMEM((NLAT, 3, 8, 128), F32),
-            pltpu.VMEM((48, 8, 128), F32),
-            pltpu.SemaphoreType.DMA((NLON,)),
-            pltpu.SemaphoreType.DMA((NLON,)),
-            pltpu.SemaphoreType.DMA((NLAT,)),
-            pltpu.SemaphoreType.DMA((NLAT,)),
-            pltpu.SemaphoreType.DMA((NLON,)),
-            pltpu.SemaphoreType.DMA((NLON,)),
-        ],
-        compiler_params=pltpu.CompilerParams(collective_id=1, has_side_effects=True),
-        name="gradient_sum",
-    )(part)
-
-
-def unpack_kernel(whole, grad1, grad2, gradh, loss):
-    packed = jnp.concatenate(
-        [jnp.concatenate([whole[6 * g + h] for h in range(6)], axis=1) for g in range(8)], axis=0)
-    packed_t = packed.T
+def unpack_kernel(whole_a, whole_b, grad1, grad2, gradh, loss):
+    packed = jnp.concatenate([whole_a[g] for g in range(NLAT)], axis=0)
+    first = jnp.concatenate([whole_b[g] for g in range(NLAT)], axis=0).T
     for t in range(9):
         grad2[t] = packed[:, 64 * t : 64 * (t + 1)]
-        grad1[t] = packed_t[576 + 16 * t : 576 + 16 * t + BANDS, :]
-    gradh[...] = packed_t[720 : 720 + NCLASS, :]
-    loss[...] = packed[0:1, 736:737]
-
-
-def unpacked(whole):
+        grad1[t] = first[16 * t : 16 * t + BANDS, :]
+    gradh[...] = packed[:, 512:640].T[64 : 64 + NCLASS, :]
+    loss[...] = packed[0:1, 592:593]
+
+
+def unpacked(whole_a, whole_b):
     return pl.pallas_call(
         unpack_kernel,
         out_shape=(
@@ -608,16 +602,16 @@
             jax.ShapeDtypeStruct((NCLASS, FEAT), F32),
             jax.ShapeDtypeStruct((1, 1), F32),
         ),
-        in_specs=[VM],
+        in_specs=[VM, VM],
         out_specs=(VM, VM, VM, VM),
         name="unpack",
-    )(whole)
+    )(whole_a, whole_b)
 
 
 def body(patches, requests, foot, widx, cw, labels, w1, w2, head):
     comp, strip = gather(patches, requests, foot.T, widx.T, cw, labels)
-    skip, part = tile_pass(comp, strip, jnp.swapaxes(w1, 1, 2), w2, head)
-    grad1, grad2, gradh, loss = unpacked(summed(part))
+    skip, whole_a, whole_b = tile_pass(comp, strip, jnp.swapaxes(w1, 1, 2), w2, head)
+    grad1, grad2, gradh, loss = unpacked(whole_a, whole_b)
     return skip, jnp.swapaxes(grad1, 1, 2), grad2, gradh, loss.reshape(())
 
 

time: 81.8 us -> 80.3 us (0.982)
  Pallas kernels: 80.7 us -> 77.2 us
  local copies, waits for them, and re-layouts: 0 us -> 2.26 us
    pallas_call x1 -> x0, Pallas kernels: 19.9 us -> none  [summed(): pl.pallas_call(sum_kernel, out_shape=jax.ShapeDtypeStruct((48, 8, 128), F...]
    pallas_call x1, Pallas kernels: 17.6 us -> 34 us  [tile_pass(): pl.pallas_call(tile_kernel, out_shape=(jax.ShapeDtypeStruct((FEAT, ROWS,...]
    unnamed x0 -> x1, local copies, waits for them, and re-layouts: none -> 2.26 us
where the time goes in v2:
time: 80.3 us; the launch traced here: 80.1 us
  Pallas kernels  77.2 us (96%)
  local copies, waits for them, and re-layouts  2.26 us (3%)
    pallas_call x1, Pallas kernels, gather(): pl.pallas_call(gather_kernel, out_shape=(jax.ShapeDtypeStruct((70, 16, 12...  41.4 us
    pallas_call x1, Pallas kernels, tile_pass(): pl.pallas_call(tile_kernel, out_shape=(jax.ShapeDtypeStruct((FEAT, ROWS,...  34 us
    unnamed x1, local copies, waits for them, and re-layouts  2.26 us
    pallas_call x1, Pallas kernels, unpacked(): pl.pallas_call(unpack_kernel, out_shape=(jax.ShapeDtypeStruct((9, BANDS,...  1.8 us

profile of v2, /device:TPU:1, one launch (start us, length us, event | category | flops | bytes accessed | tf_op | source)
XLA Modules:
  0.0 80.1 jit_solution(10329042879100846159)
XLA Ops:
  0.6 41.4 %gather_blend_halo.1 = (bf16[70,16,128]{2,1,0:T(8,128)(2,1)}, bf16[10,16,128]{2,1,0:T(8,128)(2,1)}) custom-call(bf16[192,1536]{1,0:T(8,128)(2,1)} %patches.1, s32[1,512]{1,0:T(1,128)} %requests.1, s32[8,64]{1,0:T(8,128)} %bitcast.6, s32[8,64]{1,0:T(8,128)} %bitcast.7, f32[16]{0:T(128)} %cw.1, s32[64,128]{1,0:T(8,128)} %labels.1), custom_call_target="tpu_custom_call" | custom-call | tf_op jit(solution)/shard_map/gather_blend_halo/pallas_call | solution.py:240
  42.0 34.0 %tile_forward_backward_sum.1 = (bf16[64,64,128]{2,1,0:T(8,128)(2,1)}, f32[8,8,640]{2,1,0:T(8,128)}, f32[8,8,256]{2,1,0:T(8,128)}) custom-call(bf16[70,16,128]{2,1,0:T(8,128)(2,1)} %get-tuple-element.14.comp, bf16[10,16,128]{2,1,0:T(8,128)(2,1)} %get-tuple-element.15.strip, bf16[9,12,64]{2,1,0:T(8,128)(2,1)} %bitcast.5, bf16[9,64,64]{2,1,0:T(8,128)(2,1)} %w2.1, ...), custom_call_target="tpu_custom_call" | custom-call | tf_op jit(solution)/shard_map/tile_forward_backward_sum/pallas_call | solution.py:544
  76.0 1.8 %unpack.1 = (f32[9,12,64]{2,1,0:T(8,128)}, f32[9,64,64]{2,1,0:T(8,128)}, f32[11,64]{1,0:T(8,128)}, f32[1,1]{1,0:T(1,128)}) custom-call(f32[8,8,640]{2,1,0:T(8,128)} %get-tuple-element.17.whole_a, f32[8,8,256]{2,1,0:T(8,128)} %get-tuple-element.18.whole_b), custom_call_target="tpu_custom_call" | custom-call | tf_op jit(solution)/shard_map/unpack/pallas_call | solution.py:597
  77.8 2.3 %copy.15 = bf16[64,64,128]{2,1,0:T(8,128)(2,1)} copy(bf16[64,64,128]{2,1,0:T(8,128)(2,1)} %get-tuple-element.28) | data formatting | bytes 2097152
